TPU v7x, 32 devices: a whole 2x2x4 slice. The times are simulated.
32 devices in a mesh: dp: 8 (over z, x), head: 4 (over y, core).
Axes of the slice: x: 2, y: 2, z: 4, core: 2. Of those that a mesh axis runs over, the one named last changes fastest.
Arguments:
- layer_input: bfloat16 [64, 197, 768], P(('dp', 'head')), may hold values from -6 to 6
- prompts: bfloat16 [100, 768], replicated, may hold values from -6 to 6
- lengths: int32 [64], P('dp'), may hold values from 1 to 100, as said below
- key_mask: int32 [64, 297], P('dp'), may hold values 0 or 1
- ln1_gain: float32 [768], replicated, may hold values from 0.1 to 1.9
- ln1_shift: float32 [768], replicated, may hold values from -1.5 to 1.5
- w_qkv: bfloat16 [3, 768, 768], P(None, 'dp', 'head'), may hold values from -0.3125 to 0.3125
- w_out: bfloat16 [768, 768], P('head', 'dp'), may hold values from -0.875 to 0.875
- b_out: float32 [768], replicated, may hold values from -1.5 to 1.5
- ln2_gain: float32 [768], replicated, may hold values from 0.1 to 1.9
- ln2_shift: float32 [768], replicated, may hold values from -1.5 to 1.5
- w_fc1: bfloat16 [768, 3072], P('dp', 'head'), may hold values from -0.21875 to 0.21875
- b_fc1: float32 [3072], P('head'), may hold values from -2.5 to 2.5
- w_fc2: bfloat16 [3072, 768], P('head', 'dp'), may hold values from -0.15625 to 0.15625
- b_fc2: float32 [768], replicated, may hold values from -1.5 to 1.5
- grad_output: bfloat16 [64, 297, 768], P(('dp', 'head')), may hold values from -6 to 6
Outputs:
- layer_output: bfloat16 [64, 297, 768], P(('dp', 'head'))
- grad_input: bfloat16 [64, 197, 768], P(('dp', 'head'))
- grad_prompts: float32 [100, 768], replicated
Inputs may be any that keep to these rules, and one draw needn't show every extreme that they name: `lengths`: each length is one of 1, 10, 50 and 100; both 1 and 100 occur.
All inputs are finite; a program needn't handle non-finite values. No bound on the sum of `key_mask` on one device may be relied on, other than what follows from the above.
Results may differ from a plain program's by a relative error of at most 0.019.
Values may be sent and summed in bfloat16 or wider, within the bound.
No kernel may reach another device: no remote copies, remote signals or barrier semaphores. Data moves between devices by JAX's collectives and lax.ppermute only.
A program may use at most 128 MiB of HBM per device.

v0:
```python
import jax
import jax.numpy as jnp
from jax import lax
from jax.sharding import PartitionSpec as P

HEAD_DIM = 64
IMG_TOK = 197
PROMPTS = 100
EPSILON = 1e-06


def layer_norm(rows, gain, shift):
    center = rows - jnp.mean(rows, axis=-1, keepdims=True)
    return (
        center * lax.rsqrt(jnp.mean(center * center, axis=-1, keepdims=True) + EPSILON) * gain
        + shift
    )


def token_masks(lengths, key_mask):
    position = lax.broadcasted_iota(jnp.int32, key_mask.shape, 1)
    used = (position < IMG_TOK) | (position - IMG_TOK < lengths[:, None])
    seen = (key_mask == 1) | (position == 0)
    return (used, used & seen)


def project(rows_b, weight):
    return jnp.einsum("isd,dc->isc", rows_b, weight, preferred_element_type=jnp.float32)


def attend(rows_b, full_qkv, visible):
    img_count, seq_len = (rows_b.shape[0], rows_b.shape[1])
    head_count = full_qkv.shape[2] // HEAD_DIM
    projected = jnp.einsum(
        "isd,tdc->tisc", rows_b, full_qkv, preferred_element_type=jnp.float32
    ).astype(jnp.bfloat16)
    projected = projected.reshape(3, img_count, seq_len, head_count, HEAD_DIM)
    query_rows, key_rows, value_rows = (projected[0], projected[1], projected[2])
    scores = jnp.einsum(
        "ishc,ithc->ihst", query_rows, key_rows, preferred_element_type=jnp.float32
    ) * HEAD_DIM ** (-0.5)
    scores = jnp.where(visible[:, None, None, :], scores, -1000000000.0)
    attn_probs = jax.nn.softmax(scores, axis=-1)
    return (query_rows, key_rows, value_rows, attn_probs)


def mix_values(probs_b, value_rows):
    img_count, seq_len = (value_rows.shape[0], value_rows.shape[1])
    context = jnp.einsum("ihst,ithc->ishc", probs_b, value_rows, preferred_element_type=jnp.float32)
    return context.astype(jnp.bfloat16).reshape(img_count, seq_len, value_rows.shape[2] * HEAD_DIM)


def mlp_back(grad_all, pre_act, fc1_rows, fc2_rows):
    grad_active_b = jnp.einsum(
        "isd,fd->isf", grad_all, fc2_rows, preferred_element_type=jnp.float32
    ).astype(jnp.bfloat16)
    _, gelu_back = jax.vjp(lambda values_in: jax.nn.gelu(values_in, approximate=False), pre_act)
    grad_pre_b = gelu_back(grad_active_b.astype(jnp.float32))[0].astype(jnp.bfloat16)
    return jnp.einsum("isf,df->isd", grad_pre_b, fc1_rows, preferred_element_type=jnp.float32)


def attn_back(grad_all, out_rows, qkv_rows, query_rows, key_rows, value_rows, attn_probs, probs_b):
    img_count, seq_len, head_count = (value_rows.shape[0], value_rows.shape[1], value_rows.shape[2])
    local_width = head_count * HEAD_DIM
    grad_context = jnp.einsum(
        "isd,cd->isc", grad_all, out_rows, preferred_element_type=jnp.float32
    ).astype(jnp.bfloat16)
    grad_context = grad_context.reshape(img_count, seq_len, head_count, HEAD_DIM)
    grad_value = jnp.einsum(
        "ihst,ishc->ithc", probs_b, grad_context, preferred_element_type=jnp.float32
    ).astype(jnp.bfloat16)
    grad_probs = jnp.einsum(
        "ishc,ithc->ihst", grad_context, value_rows, preferred_element_type=jnp.float32
    )
    grad_scores = (
        attn_probs * (grad_probs - jnp.sum(attn_probs * grad_probs, axis=-1, keepdims=True))
    ).astype(jnp.bfloat16)
    grad_query = (
        jnp.einsum("ihst,ithc->ishc", grad_scores, key_rows, preferred_element_type=jnp.float32)
        * HEAD_DIM ** (-0.5)
    ).astype(jnp.bfloat16)
    grad_key = (
        jnp.einsum("ihst,ishc->ithc", grad_scores, query_rows, preferred_element_type=jnp.float32)
        * HEAD_DIM ** (-0.5)
    ).astype(jnp.bfloat16)
    stacked = jnp.stack([grad_query, grad_key, grad_value]).reshape(
        3, img_count, seq_len, local_width
    )
    return jnp.einsum("tisc,tdc->isd", stacked, qkv_rows, preferred_element_type=jnp.float32)


def per_device(
    layer_input,
    prompts,
    lengths,
    key_mask,
    ln1_gain,
    ln1_shift,
    w_qkv,
    w_out,
    b_out,
    ln2_gain,
    ln2_shift,
    w_fc1,
    b_fc1,
    w_fc2,
    b_fc2,
    grad_output,
):
    own_count = layer_input.shape[0]
    model_width = layer_input.shape[2]
    offset = lax.axis_index("head") * own_count
    used_all, visible = token_masks(lengths, key_mask)
    used_own = lax.dynamic_slice_in_dim(used_all, offset, own_count, 0).astype(jnp.float32)[
        ..., None
    ]
    gain_one, shift_one = (ln1_gain, ln1_shift)
    gain_two, shift_two = (ln2_gain, ln2_shift)
    full_qkv, full_out, full_fc1, full_fc2 = (
        lax.all_gather(w_qkv, "dp", axis=1, tiled=True),
        lax.all_gather(w_out, "dp", axis=1, tiled=True),
        lax.all_gather(w_fc1, "dp", axis=0, tiled=True),
        lax.all_gather(w_fc2, "dp", axis=1, tiled=True),
    )
    prompt_rows = jnp.broadcast_to(
        prompts.astype(jnp.float32)[None], (own_count, PROMPTS, model_width)
    )
    stream = jnp.concatenate([layer_input.astype(jnp.float32), prompt_rows], axis=1)
    normed_attn, back_attn_norm = jax.vjp(
        lambda rows: layer_norm(rows, gain_one, shift_one), stream
    )
    normed_attn_b = normed_attn.astype(jnp.bfloat16)
    grad_rows = grad_output.astype(jnp.float32) * used_own
    gathered_attn = lax.all_gather(normed_attn_b, "head", axis=0, tiled=True)
    query_rows, key_rows, value_rows, attn_probs = attend(gathered_attn, full_qkv, visible)
    probs_b = attn_probs.astype(jnp.bfloat16)
    context = mix_values(probs_b, value_rows)
    attn_sum = lax.psum_scatter(
        project(context, full_out).astype(jnp.bfloat16), "head", scatter_dimension=0, tiled=True
    ).astype(jnp.float32)
    hidden_mid = stream + attn_sum + b_out
    normed_mlp, back_mlp_norm = jax.vjp(
        lambda rows: layer_norm(rows, gain_two, shift_two), hidden_mid
    )
    normed_mlp_b = normed_mlp.astype(jnp.bfloat16)
    gathered_mlp = lax.all_gather(normed_mlp_b, "head", axis=0, tiled=True)
    pre_act = project(gathered_mlp, full_fc1) + b_fc1
    active_b = jax.nn.gelu(pre_act, approximate=False).astype(jnp.bfloat16)
    mlp_sum = lax.psum_scatter(
        project(active_b, full_fc2).astype(jnp.bfloat16), "head", scatter_dimension=0, tiled=True
    ).astype(jnp.float32)
    result = ((hidden_mid + mlp_sum + b_fc2) * used_own).astype(jnp.bfloat16)
    held_inputs = lax.optimization_barrier((w_qkv, w_out, w_fc1, w_fc2, grad_rows))
    grad_rows = held_inputs[4]
    back_qkv, back_out, back_fc1, back_fc2 = (
        lax.all_gather(held_inputs[0], "dp", axis=1, tiled=True),
        lax.all_gather(held_inputs[1], "dp", axis=1, tiled=True),
        lax.all_gather(held_inputs[2], "dp", axis=0, tiled=True),
        lax.all_gather(held_inputs[3], "dp", axis=1, tiled=True),
    )
    grad_mlp_b = grad_rows.astype(jnp.bfloat16)
    grad_mlp_all, gathered_again = (
        lax.all_gather(grad_mlp_b, "head", axis=0, tiled=True),
        lax.all_gather(normed_mlp_b, "head", axis=0, tiled=True),
    )
    pre_act = project(gathered_again, back_fc1) + b_fc1
    grad_normed_mlp = lax.psum_scatter(
        mlp_back(grad_mlp_all, pre_act, back_fc1, back_fc2).astype(jnp.bfloat16),
        "head",
        scatter_dimension=0,
        tiled=True,
    ).astype(jnp.float32)
    grad_mid = grad_rows + back_mlp_norm(grad_normed_mlp)[0]
    grad_attn_b = grad_mid.astype(jnp.bfloat16)
    grad_attn_all, gathered_again = (
        lax.all_gather(grad_attn_b, "head", axis=0, tiled=True),
        lax.all_gather(normed_attn_b, "head", axis=0, tiled=True),
    )
    query_rows, key_rows, value_rows, attn_probs = attend(gathered_again, back_qkv, visible)
    probs_b = attn_probs.astype(jnp.bfloat16)
    grad_partial = attn_back(
        grad_attn_all, back_out, back_qkv, query_rows, key_rows, value_rows, attn_probs, probs_b
    )
    grad_normed_attn = lax.psum_scatter(
        grad_partial.astype(jnp.bfloat16), "head", scatter_dimension=0, tiled=True
    ).astype(jnp.float32)
    grad_stream = grad_mid + back_attn_norm(grad_normed_attn)[0]
    grad_input = grad_stream[:, :IMG_TOK].astype(jnp.bfloat16)
    grad_prompts = lax.psum(jnp.sum(grad_stream[:, IMG_TOK:], axis=0), ("dp", "head"))
    return (result, grad_input, grad_prompts)


def solution(mesh):
    placed = (
        P(("dp", "head"), None, None),
        P(),
        P("dp"),
        P("dp", None),
        P(),
        P(),
        P(None, "dp", "head"),
        P("head", "dp"),
        P(),
        P(),
        P(),
        P("dp", "head"),
        P("head"),
        P("head", "dp"),
        P(),
        P(("dp", "head"), None, None),
    )
    return jax.shard_map(
        per_device,
        mesh=mesh,
        in_specs=placed,
        out_specs=(P(("dp", "head"), None, None), P(("dp", "head"), None, None), P()),
        check_vma=False,
    )
```

profile of v0, /device:TPU:8, one launch (start us, length us, event | category | flops | bytes accessed | tf_op | source)
XLA Modules:
  0.0 717.3 jit_solution(3644398181313778874)
XLA Ops:
  12.6 36.7 %all_gather.39 = bf16[3,768,192]{2,0,1:T(4,128)(2,1)} all-gather(bf16[3,96,192]{2,0,1:T(4,128)(2,1)S(1)} %copy.34), channel_id=1, replica_groups=mesh['dp'=8,'head'=4] {'dp'}, dimensions={1}, use_global_device_ids=true | all-gather | bytes 995328 | tf_op jit(solution)/shard_map/all_gather | solution.py:120
  49.3 3.4 copy.35
  52.7 30.5 %all_gather.40 = bf16[192,768]{0,1:T(8,128)(2,1)S(1)} all-gather(bf16[192,96]{0,1:T(8,128)(2,1)S(1)} %copy.37), channel_id=1, replica_groups=mesh['dp'=8,'head'=4] {'dp'}, dimensions={1}, use_global_device_ids=true | all-gather | bytes 331776 | tf_op jit(solution)/shard_map/all_gather | solution.py:121
  83.3 5.2 convert_bitcast_fusion.1
  90.5 8.2 %fusion.168 = (f32[8,3,297]{2,1,0:T(4,128)S(1)}, f32[8,3,297,297]{2,3,1,0:T(8,128)}) fusion(pred[8,297]{1,0:T(8,128)(4,1)S(1)} %get-tuple-element.30, bf16[8,297,3,64]{1,3,2,0:T(8,128)(2,1)} %bitcast.105, bf16[8,297,3,64]{1,3,2,0:T(8,128)(2,1)} %bitcast.104), kind=kOutput, calls=%fused_computation.222 | convolution fusion | flops 279446432 | bytes 10323720 | tf_op jit(solution)/shard_map/sub | solution.py:43
  98.7 5.8 fusion.73
  104.4 3.2 convolution_convert_fusion
  110.4 41.4 %reduce-scatter.5.cloned.1.call-done = bf16[2,297,768]{2,1,0:T(8,128)(2,1)} async-done(((bf16[8,297,768]{2,1,0:T(8,128)(2,1)}), bf16[2,297,768]{2,1,0:T(8,128)(2,1)}) %reduce-scatter.5.cloned.1.call-update) | async-done | bytes 912400 | tf_op jit(solution)/shard_map/reduce_scatter | solution.py:138
  161.7 26.8 %all-gather.11.cloned.1.call-done = bf16[8,297,768]{2,1,0:T(8,128)(2,1)} async-done(((bf16[2,297,768]{2,1,0:T(8,128)(2,1)}), bf16[8,297,768]{2,1,0:T(8,128)(2,1)}) %all-gather.11.cloned.1.call-update) | async-done | bytes 3649552 | tf_op jit(solution)/shard_map/all_gather | solution.py:146
  188.5 8.4 %fusion.82 = f32[8,297,768]{2,1,0:T(8,128)} fusion(bf16[8,297,768]{2,1,0:T(8,128)(2,1)} %all-gather.11.cloned.1.call-done, bf16[768,768]{1,0:T(8,128)(2,1)} %all-gather.17.cloned.1.call-done), kind=kOutput, calls=%fused_computation.120 | convolution fusion | flops 2802843648 | bytes 12128256 | tf_op jit(solution)/shard_map/isd,dc->isc/dot_general | solution.py:28
  196.9 34.4 %all-gather.21.cloned.1.call-done = bf16[768,768]{0,1:T(8,128)(2,1)} async-done(((bf16[768,96]{0,1:T(8,128)(2,1)}), bf16[768,768]{0,1:T(8,128)(2,1)}) %all-gather.21.cloned.1.call-update) | async-done | bytes 1179664 | tf_op jit(solution)/shard_map/all_gather | solution.py:159
  231.3 32.9 %all-gather.19.cloned.1.call-done = bf16[8,297,768]{2,1,0:T(8,128)(2,1)} async-done(((bf16[2,297,768]{2,1,0:T(8,128)(2,1)}), bf16[8,297,768]{2,1,0:T(8,128)(2,1)}) %all-gather.19.cloned.1.call-update) | async-done | bytes 3649552 | tf_op jit(solution)/shard_map/all_gather | solution.py:163
  264.2 27.0 %fusion.57 = bf16[8,297,768]{2,1,0:T(8,128)(2,1)} fusion(f32[8,297,768]{2,1,0:T(8,128)} %fusion.82, f32[768]{0:T(1024)S(1)} %copy-done.35, bf16[8,297,768]{2,1,0:T(8,128)(2,1)} %all-gather.19.cloned.1.call-done, bf16[768,768]{0,1:T(8,128)(2,1)} %all-gather.21.cloned.1.call-done, bf16[768,768]{1,0:T(8,128)(2,1)} %all-gather.17.cloned.1.call-done), kind=kOutput, calls=%fused_computation.89 | convolution fusion | flops 5744369664 | bytes 16960512 | tf_op jit(solution)/shard_map/isf,df->isd/dot_general | solution.py:59
  291.2 9.2 %reduce-scatter.7.cloned.1.call-start = ((), (), s32[]{:S(2)}) async-start(), calls=%async_computation.9 | async-start | bytes 4669440 | tf_op jit(solution)/shard_map/reduce_scatter | solution.py:149
  300.4 6.6 all-gather.13.cloned.1.call-done
  307.0 10.3 %fusion.70 = (u8[297,768]{1,0:T(8,128)(4,1)S(1)}, u8[297,768]{1,0:T(8,128)(4,1)S(1)}, f32[8,297,768]{2,1,0:T(8,128)}) fusion(f32[768]{0:T(1024)S(1)} %copy-done.35, bf16[8,297,768]{2,1,0:T(8,128)(2,1)} %all-gather.11.cloned.1.call-done, bf16[768,768]{1,0:T(8,128)(2,1)} %all-gather.13.cloned.1.call-done), kind=kOutput, calls=%fused_computation.109 | convolution fusion | flops 2827934208 | bytes 12587520 | tf_op jit(solution)/shard_map/isd,dc->isc/dot_general | solution.py:28
  317.2 32.0 %all-gather.15.cloned.1.call-done = bf16[768,768]{0,1:T(8,128)(2,1)} async-done(((bf16[768,96]{0,1:T(8,128)(2,1)}), bf16[768,768]{0,1:T(8,128)(2,1)}) %all-gather.15.cloned.1.call-update) | async-done | bytes 1179664 | tf_op jit(solution)/shard_map/all_gather | solution.py:123
  349.3 23.0 %fusion.60 = bf16[8,297,768]{2,1,0:T(8,128)(2,1)} fusion(f32[8,297,768]{2,1,0:T(8,128)} %get-tuple-element.33, f32[768]{0:T(1024)S(1)} %copy-done.35, bf16[768,768]{0,1:T(8,128)(2,1)} %all-gather.15.cloned.1.call-done, u8[297,768]{1,0:T(8,128)(4,1)S(1)} %get-tuple-element.20, u8[297,768]{1,0:T(8,128)(4,1)S(1)} %get-tuple-element.19), kind=kOutput, calls=%fused_computation.90 | convolution fusion | flops 2934226944 | bytes 12587520 | tf_op jit(solution)/shard_map/isd,dc->isc/dot_general | solution.py:28
  375.4 38.2 %reduce-scatter.7.cloned.1.call-done = bf16[2,297,768]{2,1,0:T(8,128)(2,1)} async-done(((bf16[8,297,768]{2,1,0:T(8,128)(2,1)}), bf16[2,297,768]{2,1,0:T(8,128)(2,1)}) %reduce-scatter.7.cloned.1.call-update) | async-done | bytes 912400 | tf_op jit(solution)/shard_map/reduce_scatter | solution.py:149
  413.6 3.6 fusion.164
  417.5 28.5 %all_gather.49 = bf16[192,768]{0,1:T(8,128)(2,1)S(1)} all-gather(bf16[192,96]{0,1:T(8,128)(2,1)S(1)} %copy.42), channel_id=1, replica_groups=mesh['dp'=8,'head'=4] {'dp'}, dimensions={1}, use_global_device_ids=true | all-gather | bytes 331776 | tf_op jit(solution)/shard_map/all_gather | solution.py:157
  446.1 39.4 %all_gather.47 = bf16[3,768,192]{2,0,1:T(4,128)(2,1)S(1)} all-gather(bf16[3,96,192]{2,0,1:T(4,128)(2,1)S(1)} %copy.40), channel_id=1, replica_groups=mesh['dp'=8,'head'=4] {'dp'}, dimensions={1}, use_global_device_ids=true | all-gather | bytes 995328 | tf_op jit(solution)/shard_map/all_gather | solution.py:156
  485.5 7.7 %convert_bitcast_fusion = bf16[3,8,297,192]{2,3,1,0:T(8,128)(2,1)S(1)} fusion(bf16[8,297,768]{2,1,0:T(8,128)(2,1)} %all-gather.9.cloned.1.call-done, bf16[3,768,192,1]{2,0,1,3:T(4,128)(2,1)S(1)} %bitcast.101), kind=kOutput, calls=%fused_computation.84 | convolution fusion | flops 2103501312 | bytes 7271424 | tf_op jit(solution)/shard_map/isd,tdc->tisc/dot_general | solution.py:34
  495.2 8.2 %fusion.169 = (f32[8,3,297]{2,1,0:T(4,128)S(1)}, f32[8,3,297,297]{2,3,1,0:T(8,128)}) fusion(pred[8,297]{1,0:T(8,128)(4,1)S(1)} %copy-done.33, bf16[8,297,3,64]{1,3,2,0:T(8,128)(2,1)} %bitcast.98, bf16[8,297,3,64]{1,3,2,0:T(8,128)(2,1)} %bitcast.96), kind=kOutput, calls=%fused_computation.223 | convolution fusion | flops 279446432 | bytes 10323720 | tf_op jit(solution)/shard_map/sub | solution.py:43
  503.5 3.6 convolution_convert_fusion.1
  507.1 7.6 %fusion.74 = bf16[8,3,64,297]{3,2,1,0:T(8,128)(2,1)} fusion(bf16[8,297,3,64]{1,3,2,0:T(8,128)(2,1)S(1)} %bitcast.109, f32[8,3,297,297]{2,3,1,0:T(8,128)} %get-tuple-element.35, f32[8,3,297]{2,1,0:T(4,128)S(1)} %get-tuple-element.34), kind=kOutput, calls=%fused_computation.113 | convolution fusion | flops 275668288 | bytes 10321344 | tf_op jit(solution)/shard_map/ihst,ishc->ithc/dot_general | solution.py:69
  514.8 3.4 multiply_reduce_fusion
  519.9 3.3 multiply_convert_fusion.1
  525.0 5.4 bitcast_convert_fusion
  530.5 42.3 %reduce-scatter.11.cloned.1.call-done = bf16[2,297,768]{2,1,0:T(8,128)(2,1)} async-done(((bf16[8,297,768]{2,1,0:T(8,128)(2,1)}), bf16[2,297,768]{2,1,0:T(8,128)(2,1)}) %reduce-scatter.11.cloned.1.call-update) | async-done | bytes 912400 | tf_op jit(solution)/shard_map/reduce_scatter | solution.py:184
  580.4 2.8 copy.51
  585.8 122.2 %all-reduce.2.cloned.1.call-done = f32[100,768]{1,0:T(8,128)} async-done(((f32[100,768]{1,0:T(8,128)}), f32[100,768]{1,0:T(8,128)}) %all-reduce.2.cloned.1.call-update) | async-done | bytes 307216 | tf_op jit(solution)/shard_map/psum | solution.py:189
  (151 shorter events, 39.6 us)
Async XLA Ops:
  8.0 75.3 %all-gather.9.cloned.1.call-start = ((), (), s32[]{:S(2)}) async-start(), calls=%async_computation.4 | async-start | bytes 4669440 | tf_op jit(solution)/shard_map/all_gather | solution.py:134
  12.2 71.0 %copy-start.28 = (s32[8,297]{1,0:T(8,128)S(1)}, s32[8,297]{1,0:T(8,128)}, u32[]{:S(2)}) copy-start(s32[8,297]{1,0:T(8,128)} %param.19) | copy-start | bytes 28516
  12.2 71.0 %copy-start.34 = (s32[8]{0:T(128)S(1)}, s32[8]{0:T(128)}, u32[]{:S(2)}) copy-start(s32[8]{0:T(128)} %param.18) | copy-start | bytes 100
  12.2 139.5 %reduce-scatter.5.cloned.1.call-start = ((), (), s32[]{:S(2)}) async-start(), calls=%async_computation.5 | async-start | bytes 4669440 | tf_op jit(solution)/shard_map/reduce_scatter | solution.py:138
  107.7 44.1 %copy-start.12 = (f32[768]{0:T(1024)S(1)}, f32[768]{0:T(1024)}, u32[]{:S(2)}) copy-start(f32[768]{0:T(1024)} %param.24) | copy-start | bytes 9220
  107.7 54.0 %all-gather.17.cloned.1.call-start = ((), (), s32[]{:S(2)}) async-start(), calls=%async_computation.10 | async-start | bytes 1327104 | tf_op jit(solution)/shard_map/all_gather | solution.py:158
  110.3 44.8 %copy-start.17 = (f32[768]{0:T(1024)S(1)}, f32[768]{0:T(1024)}, u32[]{:S(2)}) copy-start(f32[768]{0:T(1024)} %param.25) | copy-start | bytes 9220
  110.3 44.8 %copy-start.30 = (f32[768]{0:T(1024)S(1)}, f32[768]{0:T(1024)}, u32[]{:S(2)}) copy-start(f32[768]{0:T(1024)} %param.26) | copy-start | bytes 9220
  110.3 78.1 %all-gather.11.cloned.1.call-start = ((), (), s32[]{:S(2)}) async-start(), calls=%async_computation.6 | async-start | bytes 4669440 | tf_op jit(solution)/shard_map/all_gather | solution.py:146
  156.6 74.7 %all-gather.21.cloned.1.call-start = ((), (), s32[]{:S(2)}) async-start(), calls=%async_computation.12 | async-start | bytes 1327104 | tf_op jit(solution)/shard_map/all_gather | solution.py:159
  157.2 107.0 %all-gather.19.cloned.1.call-start = ((), (), s32[]{:S(2)}) async-start(), calls=%async_computation.11 | async-start | bytes 4669440 | tf_op jit(solution)/shard_map/all_gather | solution.py:163
  159.9 147.1 %all-gather.13.cloned.1.call-start = ((), (), s32[]{:S(2)}) async-start(), calls=%async_computation.7 | async-start | bytes 1327104 | tf_op jit(solution)/shard_map/all_gather | solution.py:122
  160.6 188.6 %all-gather.15.cloned.1.call-start = ((), (), s32[]{:S(2)}) async-start(), calls=%async_computation.8 | async-start | bytes 1327104 | tf_op jit(solution)/shard_map/all_gather | solution.py:123
  161.4 102.9 %copy-start.35 = (f32[768]{0:T(1024)S(1)}, f32[768]{0:T(1024)}, u32[]{:S(2)}) copy-start(f32[768]{0:T(1024)} %param.28) | copy-start | bytes 9220
  161.4 211.0 %reduce-scatter.9.cloned.1.call-start = ((), (), s32[]{:S(2)}) async-start(), calls=%async_computation.13 | async-start | bytes 4669440 | tf_op jit(solution)/shard_map/reduce_scatter | solution.py:167
  291.2 122.4 %reduce-scatter.7.cloned.1.call-start = ((), (), s32[]{:S(2)}) async-start(), calls=%async_computation.9 | async-start | bytes 4669440 | tf_op jit(solution)/shard_map/reduce_scatter | solution.py:149
  372.3 41.3 %copy-start.23 = (f32[2,297]{1,0:T(2,128)S(1)}, f32[2,297]{1,0:T(2,128)}, u32[]{:S(2)}) copy-start(f32[2,297]{1,0:T(2,128)} %copy-done.22) | copy-start | bytes 7132
  372.3 41.3 %copy-start.31 = (f32[768]{0:T(1024)S(1)}, f32[768]{0:T(1024)}, u32[]{:S(2)}) copy-start(f32[768]{0:T(1024)} %param.30) | copy-start | bytes 9220
  372.3 131.1 %all-gather.23.cloned.1.call-start = ((), (), s32[]{:S(2)}) async-start(), calls=%async_computation.14 | async-start | bytes 4669440 | tf_op jit(solution)/shard_map/all_gather | solution.py:176
  375.4 41.9 %copy-start.14 = (bf16[192,96]{1,0:T(8,128)(2,1)S(1)}, bf16[192,96]{1,0:T(8,128)(2,1)}, u32[]{:S(2)}) copy-start(bf16[192,96]{1,0:T(8,128)(2,1)} %param.23) | copy-start | bytes 110596
  375.4 42.0 %copy-start.11 = (bf16[3,96,192]{2,1,0:T(8,128)(2,1)S(1)}, bf16[3,96,192]{2,1,0:T(8,128)(2,1)}, u32[]{:S(2)}) copy-start(bf16[3,96,192]{2,1,0:T(8,128)(2,1)} %param.22) | copy-start | bytes 331780
  417.2 155.5 %reduce-scatter.11.cloned.1.call-start = ((), (), s32[]{:S(2)}) async-start(), calls=%async_computation.15 | async-start | bytes 4669440 | tf_op jit(solution)/shard_map/reduce_scatter | solution.py:184
  485.5 7.7 %copy-start.7 = (bf16[3,768,192]{2,0,1:T(4,128)(2,1)}, bf16[3,768,192]{2,0,1:T(4,128)(2,1)S(1)}, u32[]{:S(2)}) copy-start(bf16[3,768,192]{2,0,1:T(4,128)(2,1)S(1)} %all_gather.47) | copy-start | bytes 2654212
  503.5 11.3 %slice-start = ((s8[11206656]{0:T(1024)(128)(4,1)}), s8[4194304]{0:T(1024)(128)(4,1)S(1)}, s32[]{:S(2)}) async-start(s8[11206656]{0:T(1024)(128)(4,1)} %bitcast.94), calls=%async_computation.17 | async-start | bytes 8388608
  507.1 7.7 %copy-start.37 = (bf16[8,297,192]{1,2,0:T(8,128)(2,1)}, bf16[8,297,192]{1,2,0:T(8,128)(2,1)S(1)}, u32[]{:S(2)}) copy-start(bf16[8,297,192]{1,2,0:T(8,128)(2,1)S(1)} %convolution_convert_fusion.1) | copy-start | bytes 2737156
  507.1 7.7 %slice-start.1 = ((s8[11206656]{0:T(1024)(128)(4,1)}), s8[4194304]{0:T(1024)(128)(4,1)S(1)}, s32[]{:S(2)}) async-start(s8[11206656]{0:T(1024)(128)(4,1)} %bitcast.94), calls=%async_computation.18 | async-start | bytes 8388608
  507.1 7.7 %slice-start.2 = ((s8[11206656]{0:T(1024)(128)(4,1)}), s8[2818048]{0:T(1024)(128)(4,1)S(1)}, s32[]{:S(2)}) async-start(s8[11206656]{0:T(1024)(128)(4,1)} %bitcast.94), calls=%async_computation.19 | async-start | bytes 5636096
  530.4 42.4 %copy-start.16 = (f32[2,297]{1,0:T(2,128)S(1)}, f32[2,297]{1,0:T(2,128)}, u32[]{:S(2)}) copy-start(f32[2,297]{1,0:T(2,128)} %copy-done.15) | copy-start | bytes 7132
  530.4 42.4 %copy-start.19 = (f32[768]{0:T(1024)S(1)}, f32[768]{0:T(1024)}, u32[]{:S(2)}) copy-start(f32[768]{0:T(1024)} %param.20) | copy-start | bytes 9220
  530.4 44.2 %copy-start.25 = (f32[2,297]{1,0:T(2,128)S(1)}, f32[2,297]{1,0:T(2,128)}, u32[]{:S(2)}) copy-start(f32[2,297]{1,0:T(2,128)} %copy-done.24) | copy-start | bytes 7132
  530.4 44.2 %copy-start.21 = (f32[2,297]{1,0:T(2,128)S(1)}, f32[2,297]{1,0:T(2,128)}, u32[]{:S(2)}) copy-start(f32[2,297]{1,0:T(2,128)} %copy-done.20) | copy-start | bytes 7132
  530.4 177.6 %all-reduce.2.cloned.1.call-start = ((), (), s32[]{:S(2)}) async-start(), calls=%async_computation.16 | async-start | bytes 638976 | tf_op jit(solution)/shard_map/psum | solution.py:189
  (22 other events, 58.3 us)
Sparse Core Ops, SparseCore 0:
  12.4 33.0 all-gather.8
  107.8 43.8 reduce-scatter.4
  291.3 41.6 reduce-scatter.8
  372.4 41.1 reduce-scatter.6
  580.5 127.5 all-reduce.1
Sparse Core Ops, SparseCore 1:
  110.6 42.7 all-gather.16
  156.7 31.7 all-gather.10
  190.8 40.5 all-gather.20
  233.0 31.2 all-gather.18
  266.4 40.5 all-gather.12
  309.2 40.0 all-gather.14
  417.3 31.7 all-gather.22
  530.5 42.2 reduce-scatter.10
where the time goes:
time: 726 us; the launch traced here: 717 us
  waiting for transfers between devices  379 us (52%)
  blocking collectives  135 us (19%)
  matrix products  132 us (18%)
  other arithmetic  26.4 us (4%)
  local copies, waits for them, and re-layouts  18.9 us (3%)
  between operations  16.4 us (2%)
  starting transfers between devices  9.95 us (1%)
    psum x1, waiting for transfers between devices, per_device(): lax.psum(jnp.sum(grad_stream[:, IMG_TOK:], axis=0), ('dp', 'head'))  122 us
    dot_general x4, matrix products, project(): jnp.einsum('isd,dc->isc', rows_b, weight, preferred_element_type=jnp.floa...  44.9 us
    reduce_scatter x1, waiting for transfers between devices, per_device(): lax.psum_scatter(grad_partial.astype(jnp.bfloat16), 'head', scatter_dimen...  42.3 us
    reduce_scatter x1, waiting for transfers between devices, per_device(): lax.psum_scatter(project(context, full_out).astype(jnp.bfloat16), 'head',...  41.4 us
    all_gather x1, blocking collectives, per_device(): lax.all_gather(held_inputs[0], 'dp', axis=1, tiled=True)  39.4 us
    reduce_scatter x1, waiting for transfers between devices, per_device(): lax.psum_scatter(project(active_b, full_fc2).astype(jnp.bfloat16), 'head'...  38.2 us
    all_gather x1, blocking collectives, per_device(): lax.all_gather(w_qkv, 'dp', axis=1, tiled=True)  36.7 us
    all_gather x1, waiting for transfers between devices, per_device(): lax.all_gather(held_inputs[3], 'dp', axis=1, tiled=True)  34.4 us
  transfers between devices with their start and end apart: 13, of which 9 were waited for; matrix products, arithmetic and copies ran while one was open for 15% of the time, Pallas kernels for 0%

commit v1 on v0

--- a/solution.py
+++ b/solution.py
@@ -186,7 +186,9 @@
     ).astype(jnp.float32)
     grad_stream = grad_mid + back_attn_norm(grad_normed_attn)[0]
     grad_input = grad_stream[:, :IMG_TOK].astype(jnp.bfloat16)
-    grad_prompts = lax.psum(jnp.sum(grad_stream[:, IMG_TOK:], axis=0), ("dp", "head"))
+    grad_prompts = jnp.sum(grad_stream[:, IMG_TOK:], axis=0)
+    for name in ("head", "dp"):
+        grad_prompts = lax.psum(grad_prompts, name)
     return (result, grad_input, grad_prompts)
 
 

time: 726 us -> 703 us (0.968)
  waiting for transfers between devices: 379 us -> 354 us
    psum x1 -> x2, waiting for transfers between devices: 122 us -> 97.1 us  [per_device(): grad_prompts = lax.psum(grad_prompts, name)]
  transfers between devices with their start and end apart: 13 -> 14, of which waited for: 9 -> 10; matrix products, arithmetic and copies ran while one was open for 15% -> 16% of each run, Pallas kernels for 0% -> 0%
where the time goes in v1:
time: 703 us; the launch traced here: 692 us
  waiting for transfers between devices  354 us (50%)
  blocking collectives  135 us (19%)
  matrix products  132 us (19%)
  other arithmetic  26.4 us (4%)
  local copies, waits for them, and re-layouts  18.9 us (3%)
  between operations  16.6 us (2%)
  starting transfers between devices  10 us (1%)
    psum x2, waiting for transfers between devices, per_device(): grad_prompts = lax.psum(grad_prompts, name)  97.1 us
    dot_general x4, matrix products, project(): jnp.einsum('isd,dc->isc', rows_b, weight, preferred_element_type=jnp.floa...  44.9 us
    reduce_scatter x1, waiting for transfers between devices, per_device(): lax.psum_scatter(grad_partial.astype(jnp.bfloat16), 'head', scatter_dimen...  42.3 us
    reduce_scatter x1, waiting for transfers between devices, per_device(): lax.psum_scatter(project(context, full_out).astype(jnp.bfloat16), 'head',...  41.4 us
    all_gather x1, blocking collectives, per_device(): lax.all_gather(held_inputs[0], 'dp', axis=1, tiled=True)  39.4 us
    reduce_scatter x1, waiting for transfers between devices, per_device(): lax.psum_scatter(project(active_b, full_fc2).astype(jnp.bfloat16), 'head'...  38.2 us
    all_gather x1, blocking collectives, per_device(): lax.all_gather(w_qkv, 'dp', axis=1, tiled=True)  36.7 us
    all_gather x1, waiting for transfers between devices, per_device(): lax.all_gather(held_inputs[3], 'dp', axis=1, tiled=True)  34.4 us
  transfers between devices with their start and end apart: 14, of which 10 were waited for; matrix products, arithmetic and copies ran while one was open for 16% of the time, Pallas kernels for 0%

profile of v1, /device:TPU:8, one launch (start us, length us, event | category | flops | bytes accessed | tf_op | source)
XLA Modules:
  0.0 692.5 jit_solution(13497543393800033907)
XLA Ops:
  12.6 36.7 %all_gather.39 = bf16[3,768,192]{2,0,1:T(4,128)(2,1)} all-gather(bf16[3,96,192]{2,0,1:T(4,128)(2,1)S(1)} %copy.34), channel_id=1, replica_groups=mesh['dp'=8,'head'=4] {'dp'}, dimensions={1}, use_global_device_ids=true | all-gather | bytes 995328 | tf_op jit(solution)/shard_map/all_gather | solution.py:120
  49.3 3.4 copy.35
  52.7 30.5 %all_gather.40 = bf16[192,768]{0,1:T(8,128)(2,1)S(1)} all-gather(bf16[192,96]{0,1:T(8,128)(2,1)S(1)} %copy.37), channel_id=1, replica_groups=mesh['dp'=8,'head'=4] {'dp'}, dimensions={1}, use_global_device_ids=true | all-gather | bytes 331776 | tf_op jit(solution)/shard_map/all_gather | solution.py:121
  83.3 5.2 convert_bitcast_fusion.1
  90.5 8.2 %fusion.168 = (f32[8,3,297]{2,1,0:T(4,128)S(1)}, f32[8,3,297,297]{2,3,1,0:T(8,128)}) fusion(pred[8,297]{1,0:T(8,128)(4,1)S(1)} %get-tuple-element.30, bf16[8,297,3,64]{1,3,2,0:T(8,128)(2,1)} %bitcast.105, bf16[8,297,3,64]{1,3,2,0:T(8,128)(2,1)} %bitcast.104), kind=kOutput, calls=%fused_computation.222 | convolution fusion | flops 279446432 | bytes 10323720 | tf_op jit(solution)/shard_map/sub | solution.py:43
  98.7 5.8 fusion.73
  104.4 3.2 convolution_convert_fusion
  110.4 41.4 %reduce-scatter.5.cloned.1.call-done = bf16[2,297,768]{2,1,0:T(8,128)(2,1)} async-done(((bf16[8,297,768]{2,1,0:T(8,128)(2,1)}), bf16[2,297,768]{2,1,0:T(8,128)(2,1)}) %reduce-scatter.5.cloned.1.call-update) | async-done | bytes 912400 | tf_op jit(solution)/shard_map/reduce_scatter | solution.py:138
  161.7 26.8 %all-gather.11.cloned.1.call-done = bf16[8,297,768]{2,1,0:T(8,128)(2,1)} async-done(((bf16[2,297,768]{2,1,0:T(8,128)(2,1)}), bf16[8,297,768]{2,1,0:T(8,128)(2,1)}) %all-gather.11.cloned.1.call-update) | async-done | bytes 3649552 | tf_op jit(solution)/shard_map/all_gather | solution.py:146
  188.5 8.4 %fusion.82 = f32[8,297,768]{2,1,0:T(8,128)} fusion(bf16[8,297,768]{2,1,0:T(8,128)(2,1)} %all-gather.11.cloned.1.call-done, bf16[768,768]{1,0:T(8,128)(2,1)} %all-gather.17.cloned.1.call-done), kind=kOutput, calls=%fused_computation.120 | convolution fusion | flops 2802843648 | bytes 12128256 | tf_op jit(solution)/shard_map/isd,dc->isc/dot_general | solution.py:28
  196.9 34.4 %all-gather.21.cloned.1.call-done = bf16[768,768]{0,1:T(8,128)(2,1)} async-done(((bf16[768,96]{0,1:T(8,128)(2,1)}), bf16[768,768]{0,1:T(8,128)(2,1)}) %all-gather.21.cloned.1.call-update) | async-done | bytes 1179664 | tf_op jit(solution)/shard_map/all_gather | solution.py:159
  231.3 32.9 %all-gather.19.cloned.1.call-done = bf16[8,297,768]{2,1,0:T(8,128)(2,1)} async-done(((bf16[2,297,768]{2,1,0:T(8,128)(2,1)}), bf16[8,297,768]{2,1,0:T(8,128)(2,1)}) %all-gather.19.cloned.1.call-update) | async-done | bytes 3649552 | tf_op jit(solution)/shard_map/all_gather | solution.py:163
  264.2 27.0 %fusion.57 = bf16[8,297,768]{2,1,0:T(8,128)(2,1)} fusion(f32[8,297,768]{2,1,0:T(8,128)} %fusion.82, f32[768]{0:T(1024)S(1)} %copy-done.35, bf16[8,297,768]{2,1,0:T(8,128)(2,1)} %all-gather.19.cloned.1.call-done, bf16[768,768]{0,1:T(8,128)(2,1)} %all-gather.21.cloned.1.call-done, bf16[768,768]{1,0:T(8,128)(2,1)} %all-gather.17.cloned.1.call-done), kind=kOutput, calls=%fused_computation.89 | convolution fusion | flops 5744369664 | bytes 16960512 | tf_op jit(solution)/shard_map/isf,df->isd/dot_general | solution.py:59
  291.2 9.2 %reduce-scatter.7.cloned.1.call-start = ((), (), s32[]{:S(2)}) async-start(), calls=%async_computation.9 | async-start | bytes 4669440 | tf_op jit(solution)/shard_map/reduce_scatter | solution.py:149
  300.4 6.6 all-gather.13.cloned.1.call-done
  307.0 10.3 %fusion.70 = (u8[297,768]{1,0:T(8,128)(4,1)S(1)}, u8[297,768]{1,0:T(8,128)(4,1)S(1)}, f32[8,297,768]{2,1,0:T(8,128)}) fusion(f32[768]{0:T(1024)S(1)} %copy-done.35, bf16[8,297,768]{2,1,0:T(8,128)(2,1)} %all-gather.11.cloned.1.call-done, bf16[768,768]{1,0:T(8,128)(2,1)} %all-gather.13.cloned.1.call-done), kind=kOutput, calls=%fused_computation.109 | convolution fusion | flops 2827934208 | bytes 12587520 | tf_op jit(solution)/shard_map/isd,dc->isc/dot_general | solution.py:28
  317.2 32.0 %all-gather.15.cloned.1.call-done = bf16[768,768]{0,1:T(8,128)(2,1)} async-done(((bf16[768,96]{0,1:T(8,128)(2,1)}), bf16[768,768]{0,1:T(8,128)(2,1)}) %all-gather.15.cloned.1.call-update) | async-done | bytes 1179664 | tf_op jit(solution)/shard_map/all_gather | solution.py:123
  349.3 23.0 %fusion.60 = bf16[8,297,768]{2,1,0:T(8,128)(2,1)} fusion(f32[8,297,768]{2,1,0:T(8,128)} %get-tuple-element.33, f32[768]{0:T(1024)S(1)} %copy-done.35, bf16[768,768]{0,1:T(8,128)(2,1)} %all-gather.15.cloned.1.call-done, u8[297,768]{1,0:T(8,128)(4,1)S(1)} %get-tuple-element.20, u8[297,768]{1,0:T(8,128)(4,1)S(1)} %get-tuple-element.19), kind=kOutput, calls=%fused_computation.90 | convolution fusion | flops 2934226944 | bytes 12587520 | tf_op jit(solution)/shard_map/isd,dc->isc/dot_general | solution.py:28
  375.4 38.2 %reduce-scatter.7.cloned.1.call-done = bf16[2,297,768]{2,1,0:T(8,128)(2,1)} async-done(((bf16[8,297,768]{2,1,0:T(8,128)(2,1)}), bf16[2,297,768]{2,1,0:T(8,128)(2,1)}) %reduce-scatter.7.cloned.1.call-update) | async-done | bytes 912400 | tf_op jit(solution)/shard_map/reduce_scatter | solution.py:149
  413.6 3.6 fusion.164
  417.5 28.5 %all_gather.49 = bf16[192,768]{0,1:T(8,128)(2,1)S(1)} all-gather(bf16[192,96]{0,1:T(8,128)(2,1)S(1)} %copy.42), channel_id=1, replica_groups=mesh['dp'=8,'head'=4] {'dp'}, dimensions={1}, use_global_device_ids=true | all-gather | bytes 331776 | tf_op jit(solution)/shard_map/all_gather | solution.py:157
  446.1 39.4 %all_gather.47 = bf16[3,768,192]{2,0,1:T(4,128)(2,1)S(1)} all-gather(bf16[3,96,192]{2,0,1:T(4,128)(2,1)S(1)} %copy.40), channel_id=1, replica_groups=mesh['dp'=8,'head'=4] {'dp'}, dimensions={1}, use_global_device_ids=true | all-gather | bytes 995328 | tf_op jit(solution)/shard_map/all_gather | solution.py:156
  485.5 7.7 %convert_bitcast_fusion = bf16[3,8,297,192]{2,3,1,0:T(8,128)(2,1)S(1)} fusion(bf16[8,297,768]{2,1,0:T(8,128)(2,1)} %all-gather.9.cloned.1.call-done, bf16[3,768,192,1]{2,0,1,3:T(4,128)(2,1)S(1)} %bitcast.101), kind=kOutput, calls=%fused_computation.84 | convolution fusion | flops 2103501312 | bytes 7271424 | tf_op jit(solution)/shard_map/isd,tdc->tisc/dot_general | solution.py:34
  495.2 8.2 %fusion.169 = (f32[8,3,297]{2,1,0:T(4,128)S(1)}, f32[8,3,297,297]{2,3,1,0:T(8,128)}) fusion(pred[8,297]{1,0:T(8,128)(4,1)S(1)} %copy-done.33, bf16[8,297,3,64]{1,3,2,0:T(8,128)(2,1)} %bitcast.98, bf16[8,297,3,64]{1,3,2,0:T(8,128)(2,1)} %bitcast.96), kind=kOutput, calls=%fused_computation.223 | convolution fusion | flops 279446432 | bytes 10323720 | tf_op jit(solution)/shard_map/sub | solution.py:43
  503.5 3.6 convolution_convert_fusion.1
  507.1 7.6 %fusion.74 = bf16[8,3,64,297]{3,2,1,0:T(8,128)(2,1)} fusion(bf16[8,297,3,64]{1,3,2,0:T(8,128)(2,1)S(1)} %bitcast.109, f32[8,3,297,297]{2,3,1,0:T(8,128)} %get-tuple-element.35, f32[8,3,297]{2,1,0:T(4,128)S(1)} %get-tuple-element.34), kind=kOutput, calls=%fused_computation.113 | convolution fusion | flops 275668288 | bytes 10321344 | tf_op jit(solution)/shard_map/ihst,ishc->ithc/dot_general | solution.py:69
  514.8 3.4 multiply_reduce_fusion
  519.9 3.3 multiply_convert_fusion.1
  525.0 5.4 bitcast_convert_fusion
  530.5 42.3 %reduce-scatter.11.cloned.1.call-done = bf16[2,297,768]{2,1,0:T(8,128)(2,1)} async-done(((bf16[8,297,768]{2,1,0:T(8,128)(2,1)}), bf16[2,297,768]{2,1,0:T(8,128)(2,1)}) %reduce-scatter.11.cloned.1.call-update) | async-done | bytes 912400 | tf_op jit(solution)/shard_map/reduce_scatter | solution.py:184
  580.4 32.2 %all-reduce.3.cloned.1.call-done = f32[100,768]{1,0:T(8,128)} async-done(((f32[100,768]{1,0:T(8,128)}), f32[100,768]{1,0:T(8,128)}) %all-reduce.3.cloned.1.call-update) | async-done | bytes 307216 | tf_op jit(solution)/shard_map/psum | solution.py:191
  618.1 64.9 %all-reduce.5.cloned.1.call-done = f32[100,768]{1,0:T(8,128)} async-done(((f32[100,768]{1,0:T(8,128)}), f32[100,768]{1,0:T(8,128)}) %all-reduce.5.cloned.1.call-update) | async-done | bytes 307216 | tf_op jit(solution)/shard_map/psum | solution.py:191
  (154 shorter events, 42.5 us)
Async XLA Ops:
  8.0 75.3 %all-gather.9.cloned.1.call-start = ((), (), s32[]{:S(2)}) async-start(), calls=%async_computation.4 | async-start | bytes 4669440 | tf_op jit(solution)/shard_map/all_gather | solution.py:134
  12.2 71.0 %copy-start.28 = (s32[8,297]{1,0:T(8,128)S(1)}, s32[8,297]{1,0:T(8,128)}, u32[]{:S(2)}) copy-start(s32[8,297]{1,0:T(8,128)} %param.19) | copy-start | bytes 28516
  12.2 71.0 %copy-start.34 = (s32[8]{0:T(128)S(1)}, s32[8]{0:T(128)}, u32[]{:S(2)}) copy-start(s32[8]{0:T(128)} %param.18) | copy-start | bytes 100
  12.2 139.5 %reduce-scatter.5.cloned.1.call-start = ((), (), s32[]{:S(2)}) async-start(), calls=%async_computation.5 | async-start | bytes 4669440 | tf_op jit(solution)/shard_map/reduce_scatter | solution.py:138
  107.7 44.1 %copy-start.12 = (f32[768]{0:T(1024)S(1)}, f32[768]{0:T(1024)}, u32[]{:S(2)}) copy-start(f32[768]{0:T(1024)} %param.24) | copy-start | bytes 9220
  107.7 54.0 %all-gather.17.cloned.1.call-start = ((), (), s32[]{:S(2)}) async-start(), calls=%async_computation.10 | async-start | bytes 1327104 | tf_op jit(solution)/shard_map/all_gather | solution.py:158
  110.3 44.8 %copy-start.17 = (f32[768]{0:T(1024)S(1)}, f32[768]{0:T(1024)}, u32[]{:S(2)}) copy-start(f32[768]{0:T(1024)} %param.25) | copy-start | bytes 9220
  110.3 44.8 %copy-start.30 = (f32[768]{0:T(1024)S(1)}, f32[768]{0:T(1024)}, u32[]{:S(2)}) copy-start(f32[768]{0:T(1024)} %param.26) | copy-start | bytes 9220
  110.3 78.1 %all-gather.11.cloned.1.call-start = ((), (), s32[]{:S(2)}) async-start(), calls=%async_computation.6 | async-start | bytes 4669440 | tf_op jit(solution)/shard_map/all_gather | solution.py:146
  156.6 74.7 %all-gather.21.cloned.1.call-start = ((), (), s32[]{:S(2)}) async-start(), calls=%async_computation.12 | async-start | bytes 1327104 | tf_op jit(solution)/shard_map/all_gather | solution.py:159
  157.2 107.0 %all-gather.19.cloned.1.call-start = ((), (), s32[]{:S(2)}) async-start(), calls=%async_computation.11 | async-start | bytes 4669440 | tf_op jit(solution)/shard_map/all_gather | solution.py:163
  159.9 147.1 %all-gather.13.cloned.1.call-start = ((), (), s32[]{:S(2)}) async-start(), calls=%async_computation.7 | async-start | bytes 1327104 | tf_op jit(solution)/shard_map/all_gather | solution.py:122
  160.6 188.6 %all-gather.15.cloned.1.call-start = ((), (), s32[]{:S(2)}) async-start(), calls=%async_computation.8 | async-start | bytes 1327104 | tf_op jit(solution)/shard_map/all_gather | solution.py:123
  161.4 102.9 %copy-start.35 = (f32[768]{0:T(1024)S(1)}, f32[768]{0:T(1024)}, u32[]{:S(2)}) copy-start(f32[768]{0:T(1024)} %param.28) | copy-start | bytes 9220
  161.4 211.0 %reduce-scatter.9.cloned.1.call-start = ((), (), s32[]{:S(2)}) async-start(), calls=%async_computation.13 | async-start | bytes 4669440 | tf_op jit(solution)/shard_map/reduce_scatter | solution.py:167
  291.2 122.4 %reduce-scatter.7.cloned.1.call-start = ((), (), s32[]{:S(2)}) async-start(), calls=%async_computation.9 | async-start | bytes 4669440 | tf_op jit(solution)/shard_map/reduce_scatter | solution.py:149
  372.3 41.3 %copy-start.23 = (f32[2,297]{1,0:T(2,128)S(1)}, f32[2,297]{1,0:T(2,128)}, u32[]{:S(2)}) copy-start(f32[2,297]{1,0:T(2,128)} %copy-done.22) | copy-start | bytes 7132
  372.3 41.3 %copy-start.31 = (f32[768]{0:T(1024)S(1)}, f32[768]{0:T(1024)}, u32[]{:S(2)}) copy-start(f32[768]{0:T(1024)} %param.30) | copy-start | bytes 9220
  372.3 131.1 %all-gather.23.cloned.1.call-start = ((), (), s32[]{:S(2)}) async-start(), calls=%async_computation.14 | async-start | bytes 4669440 | tf_op jit(solution)/shard_map/all_gather | solution.py:176
  375.4 41.9 %copy-start.14 = (bf16[192,96]{1,0:T(8,128)(2,1)S(1)}, bf16[192,96]{1,0:T(8,128)(2,1)}, u32[]{:S(2)}) copy-start(bf16[192,96]{1,0:T(8,128)(2,1)} %param.23) | copy-start | bytes 110596
  375.4 42.0 %copy-start.11 = (bf16[3,96,192]{2,1,0:T(8,128)(2,1)S(1)}, bf16[3,96,192]{2,1,0:T(8,128)(2,1)}, u32[]{:S(2)}) copy-start(bf16[3,96,192]{2,1,0:T(8,128)(2,1)} %param.22) | copy-start | bytes 331780
  417.2 155.5 %reduce-scatter.11.cloned.1.call-start = ((), (), s32[]{:S(2)}) async-start(), calls=%async_computation.15 | async-start | bytes 4669440 | tf_op jit(solution)/shard_map/reduce_scatter | solution.py:184
  485.5 7.7 %copy-start.7 = (bf16[3,768,192]{2,0,1:T(4,128)(2,1)}, bf16[3,768,192]{2,0,1:T(4,128)(2,1)S(1)}, u32[]{:S(2)}) copy-start(bf16[3,768,192]{2,0,1:T(4,128)(2,1)S(1)} %all_gather.47) | copy-start | bytes 2654212
  503.5 11.3 %slice-start = ((s8[11206656]{0:T(1024)(128)(4,1)}), s8[4194304]{0:T(1024)(128)(4,1)S(1)}, s32[]{:S(2)}) async-start(s8[11206656]{0:T(1024)(128)(4,1)} %bitcast.94), calls=%async_computation.18 | async-start | bytes 8388608
  507.1 7.7 %copy-start.37 = (bf16[8,297,192]{1,2,0:T(8,128)(2,1)}, bf16[8,297,192]{1,2,0:T(8,128)(2,1)S(1)}, u32[]{:S(2)}) copy-start(bf16[8,297,192]{1,2,0:T(8,128)(2,1)S(1)} %convolution_convert_fusion.1) | copy-start | bytes 2737156
  507.1 7.7 %slice-start.1 = ((s8[11206656]{0:T(1024)(128)(4,1)}), s8[4194304]{0:T(1024)(128)(4,1)S(1)}, s32[]{:S(2)}) async-start(s8[11206656]{0:T(1024)(128)(4,1)} %bitcast.94), calls=%async_computation.19 | async-start | bytes 8388608
  530.4 42.4 %copy-start.16 = (f32[2,297]{1,0:T(2,128)S(1)}, f32[2,297]{1,0:T(2,128)}, u32[]{:S(2)}) copy-start(f32[2,297]{1,0:T(2,128)} %copy-done.15) | copy-start | bytes 7132
  530.4 42.4 %copy-start.19 = (f32[768]{0:T(1024)S(1)}, f32[768]{0:T(1024)}, u32[]{:S(2)}) copy-start(f32[768]{0:T(1024)} %param.20) | copy-start | bytes 9220
  530.4 44.2 %copy-start.25 = (f32[2,297]{1,0:T(2,128)S(1)}, f32[2,297]{1,0:T(2,128)}, u32[]{:S(2)}) copy-start(f32[2,297]{1,0:T(2,128)} %copy-done.24) | copy-start | bytes 7132
  530.4 44.2 %copy-start.21 = (f32[2,297]{1,0:T(2,128)S(1)}, f32[2,297]{1,0:T(2,128)}, u32[]{:S(2)}) copy-start(f32[2,297]{1,0:T(2,128)} %copy-done.20) | copy-start | bytes 7132
  530.4 82.2 %all-reduce.3.cloned.1.call-start = ((), (), s32[]{:S(2)}) async-start(), calls=%async_computation.16 | async-start | bytes 638976 | tf_op jit(solution)/shard_map/psum | solution.py:191
  580.4 102.6 %all-reduce.5.cloned.1.call-start = ((), (), s32[]{:S(2)}) async-start(), calls=%async_computation.17 | async-start | bytes 638976 | tf_op jit(solution)/shard_map/psum | solution.py:191
  (23 other events, 65.9 us)
Sparse Core Ops, SparseCore 0:
  12.4 33.0 all-gather.8
  107.8 43.8 reduce-scatter.4
  291.3 41.6 reduce-scatter.8
  372.4 41.1 reduce-scatter.6
  580.5 32.1 all-reduce.2
Sparse Core Ops, SparseCore 1:
  110.6 42.7 all-gather.16
  156.7 31.7 all-gather.10
  190.8 40.5 all-gather.20
  233.0 31.2 all-gather.18
  266.4 40.5 all-gather.12
  309.2 40.0 all-gather.14
  417.3 31.7 all-gather.22
  530.5 42.2 reduce-scatter.10
  612.7 70.2 all-reduce.4
